TPU v7x, 512 devices: a whole 4x8x8 slice. The times are simulated.
512 devices in a mesh: pa: 8 (over y), pb: 64 (over z, x, core).
Axes of the slice: x: 4, y: 8, z: 8, core: 2. Of those that a mesh axis runs over, the one named last changes fastest.
Arguments:
- matrix: bfloat16 [12288, 24576], P('pa', 'pb'), may hold values from -6 to 6
- panels: bfloat16 [6, 12288, 128], P(None, ('pa', 'pb')), may hold values from -0.25 to 0.25
- inverses: float32 [6, 128, 128], replicated, as said below
- pivots: int32 [6, 128], replicated, may hold values from 128 to 12287, as said below
Outputs:
- factored: bfloat16 [12288, 24576], P('pa', 'pb')
Inputs may be any that keep to these rules, and one draw needn't show every extreme that they name: `pivots`: row k lists 128 different row numbers, each at least (k + 1) * 128. `inverses`: each block is unit lower triangular.
All inputs are finite; a program needn't handle non-finite values.
Results may differ from a plain program's by a relative error of at most 0.0082.
Values may be sent and summed in bfloat16 or wider, within the bound.
No kernel may reach another device: no remote copies, remote signals or barrier semaphores. Data moves between devices by JAX's collectives and lax.ppermute only.
A program may use at most 64 MiB of HBM per device.

v0:
```python
import jax
import jax.numpy as jnp
from jax import lax
from jax.sharding import PartitionSpec as P

NB = 128
STEPS = 6


def broadcast(x, axis, root):
    mine = lax.axis_index(axis) == root
    return lax.psum(jnp.where(mine, x, jnp.zeros_like(x)), axis)


def per_device(matrix, panels, inverses, pivots):
    local_rows = matrix.shape[0]
    proc_row = lax.axis_index("pa")
    first_row = proc_row * local_rows
    is_owner = proc_row == 0
    global_rows = first_row + jnp.arange(local_rows, dtype=jnp.int32)
    for step in range(STEPS):
        lo = step * NB
        hi = lo + NB
        chosen = pivots[step]
        local_idx = chosen - first_row
        owned = (local_idx >= 0) & (local_idx < local_rows)
        safe_idx = jnp.clip(local_idx, 0, local_rows - 1)
        candidates = jnp.where(
            owned[:, None], jnp.take(matrix, safe_idx, axis=0), jnp.zeros((), jnp.bfloat16)
        )
        top_local = matrix[lo:hi]
        new_top = lax.psum(candidates, "pa").astype(jnp.float32).astype(jnp.bfloat16)
        upper_here = jnp.dot(
            inverses[step],
            new_top.astype(jnp.float32),
            precision=lax.Precision.HIGHEST,
            preferred_element_type=jnp.float32,
        ).astype(jnp.bfloat16)
        upper, old_top = (broadcast(upper_here, "pa", 0), broadcast(top_local, "pa", 0))
        target = jnp.where(owned, local_idx, local_rows)
        matrix = matrix.at[target].set(old_top, mode="drop")
        product = jnp.dot(
            lax.all_gather(panels[step], "pb", axis=0, tiled=True),
            upper,
            preferred_element_type=jnp.float32,
        )
        updated = (matrix.astype(jnp.float32) - product).astype(jnp.bfloat16)
        matrix = jnp.where((global_rows >= hi)[:, None], updated, matrix)
        matrix = matrix.at[lo:hi].set(jnp.where(is_owner, upper, matrix[lo:hi]))
    return matrix


def solution(mesh):
    in_specs = (P("pa", "pb"), P(None, ("pa", "pb"), None), P(), P())
    out_specs = P("pa", "pb")
    return jax.shard_map(
        per_device, mesh=mesh, in_specs=in_specs, out_specs=out_specs, check_vma=False
    )
```

profile of v0, /device:TPU:2, one launch (start us, length us, event | category | flops | bytes accessed | tf_op | source)
XLA Modules:
  0.0 992.1 jit_solution(16481884863507782826)
XLA Ops:
  6.5 1.3 copy.89
  15.7 57.5 %all-gather = bf16[1,1536,128]{2,1,0:T(8,128)(2,1)} all-gather(bf16[1,24,128]{2,1,0:T(8,128)(2,1)S(1)} %get-tuple-element.106), channel_id=2, replica_groups=mesh['pa'=8,'pb'=64] {'pb'}, dimensions={1}, use_global_device_ids=true | all-gather | bytes 399360 | tf_op jit(solution)/shard_map/all_gather | solution.py:43
  73.2 19.3 %all-reduce.19.cloned.1.call-done = bf16[128,384]{0,1:T(8,128)(2,1)} async-done(((bf16[128,384]{0,1:T(8,128)(2,1)}), bf16[128,384]{0,1:T(8,128)(2,1)}) %all-reduce.19.cloned.1.call-update) | async-done | bytes 98320 | tf_op jit(solution)/shard_map/psum | solution.py:32
  92.5 1.8 fusion.19
  95.0 75.9 %all-reduce.41.cloned.1.call-done = (bf16[128,384]{0,1:T(8,128)(2,1)}, bf16[128,384]{0,1:T(8,128)(2,1)}) async-done(((bf16[128,384]{0,1:T(8,128)(2,1)}, bf16[128,384]{0,1:T(8,128)(2,1)}), (bf16[128,384]{0,1:T(8,128)(2,1)}, bf16[128,384]{0,1:T(8,128)(2,1)})) %all-reduce.41.cloned.1.call-update) | async-done | bytes 196624 | tf_op jit(solution)/shard_map/psum | solution.py:12
  170.9 1.0 copy.22
  171.9 1.7 scatter_fusion
  174.3 1.5 fusion.17
  176.7 1.0 gather_fusion.1
  179.2 75.1 %all-reduce.21.cloned.1.call-done = bf16[128,384]{0,1:T(8,128)(2,1)} async-done(((bf16[128,384]{0,1:T(8,128)(2,1)}), bf16[128,384]{0,1:T(8,128)(2,1)}) %all-reduce.21.cloned.1.call-update) | async-done | bytes 98320 | tf_op jit(solution)/shard_map/psum | solution.py:32
  254.4 1.8 fusion.21
  256.2 53.6 %all-gather.1 = bf16[1,1536,128]{2,1,0:T(8,128)(2,1)} all-gather(bf16[1,24,128]{2,1,0:T(8,128)(2,1)S(1)} %copy-done.9), channel_id=3, replica_groups=mesh['pa'=8,'pb'=64] {'pb'}, dimensions={1}, use_global_device_ids=true | all-gather | bytes 399360 | tf_op jit(solution)/shard_map/all_gather | solution.py:43
  310.5 22.2 %all-reduce.39.cloned.1.call-done = (bf16[128,384]{0,1:T(8,128)(2,1)}, bf16[128,384]{0,1:T(8,128)(2,1)}) async-done(((bf16[128,384]{0,1:T(8,128)(2,1)}, bf16[128,384]{0,1:T(8,128)(2,1)}), (bf16[128,384]{0,1:T(8,128)(2,1)}, bf16[128,384]{0,1:T(8,128)(2,1)})) %all-reduce.39.cloned.1.call-update) | async-done | bytes 196624 | tf_op jit(solution)/shard_map/psum | solution.py:12
  332.6 1.0 copy.27
  333.6 1.7 scatter_fusion.1
  336.1 1.5 fusion.16
  338.5 1.0 gather_fusion.2
  341.0 75.2 %all-reduce.23.cloned.1.call-done = bf16[128,384]{0,1:T(8,128)(2,1)} async-done(((bf16[128,384]{0,1:T(8,128)(2,1)}), bf16[128,384]{0,1:T(8,128)(2,1)}) %all-reduce.23.cloned.1.call-update) | async-done | bytes 98320 | tf_op jit(solution)/shard_map/psum | solution.py:32
  416.1 1.8 fusion.23
  418.0 53.8 %all-gather.2 = bf16[1,1536,128]{2,1,0:T(8,128)(2,1)} all-gather(bf16[1,24,128]{2,1,0:T(8,128)(2,1)S(1)} %copy-done.8), channel_id=4, replica_groups=mesh['pa'=8,'pb'=64] {'pb'}, dimensions={1}, use_global_device_ids=true | all-gather | bytes 399360 | tf_op jit(solution)/shard_map/all_gather | solution.py:43
  472.4 22.0 %all-reduce.37.cloned.1.call-done = (bf16[128,384]{0,1:T(8,128)(2,1)}, bf16[128,384]{0,1:T(8,128)(2,1)}) async-done(((bf16[128,384]{0,1:T(8,128)(2,1)}, bf16[128,384]{0,1:T(8,128)(2,1)}), (bf16[128,384]{0,1:T(8,128)(2,1)}, bf16[128,384]{0,1:T(8,128)(2,1)})) %all-reduce.37.cloned.1.call-update) | async-done | bytes 196624 | tf_op jit(solution)/shard_map/psum | solution.py:12
  494.4 1.0 copy.33
  495.4 1.7 scatter_fusion.2
  497.8 1.5 fusion.15
  500.2 1.0 gather_fusion.3
  502.7 75.2 %all-reduce.25.cloned.1.call-done = bf16[128,384]{0,1:T(8,128)(2,1)} async-done(((bf16[128,384]{0,1:T(8,128)(2,1)}), bf16[128,384]{0,1:T(8,128)(2,1)}) %all-reduce.25.cloned.1.call-update) | async-done | bytes 98320 | tf_op jit(solution)/shard_map/psum | solution.py:32
  577.9 1.8 fusion.25
  579.7 53.6 %all-gather.3 = bf16[1,1536,128]{2,1,0:T(8,128)(2,1)} all-gather(bf16[1,24,128]{2,1,0:T(8,128)(2,1)S(1)} %copy-done.7), channel_id=5, replica_groups=mesh['pa'=8,'pb'=64] {'pb'}, dimensions={1}, use_global_device_ids=true | all-gather | bytes 399360 | tf_op jit(solution)/shard_map/all_gather | solution.py:43
  633.9 22.3 %all-reduce.35.cloned.1.call-done = (bf16[128,384]{0,1:T(8,128)(2,1)}, bf16[128,384]{0,1:T(8,128)(2,1)}) async-done(((bf16[128,384]{0,1:T(8,128)(2,1)}, bf16[128,384]{0,1:T(8,128)(2,1)}), (bf16[128,384]{0,1:T(8,128)(2,1)}, bf16[128,384]{0,1:T(8,128)(2,1)})) %all-reduce.35.cloned.1.call-update) | async-done | bytes 196624 | tf_op jit(solution)/shard_map/psum | solution.py:12
  656.2 1.0 copy.39
  657.3 1.7 scatter_fusion.3
  659.7 1.5 fusion.14
  662.1 1.0 gather_fusion.4
  664.6 75.1 %all-reduce.27.cloned.1.call-done = bf16[128,384]{0,1:T(8,128)(2,1)} async-done(((bf16[128,384]{0,1:T(8,128)(2,1)}), bf16[128,384]{0,1:T(8,128)(2,1)}) %all-reduce.27.cloned.1.call-update) | async-done | bytes 98320 | tf_op jit(solution)/shard_map/psum | solution.py:32
  739.7 1.8 fusion.27
  741.6 53.8 %all-gather.4 = bf16[1,1536,128]{2,1,0:T(8,128)(2,1)} all-gather(bf16[1,24,128]{2,1,0:T(8,128)(2,1)S(1)} %get-tuple-element.107), channel_id=6, replica_groups=mesh['pa'=8,'pb'=64] {'pb'}, dimensions={1}, use_global_device_ids=true | all-gather | bytes 399360 | tf_op jit(solution)/shard_map/all_gather | solution.py:43
  795.4 22.5 %all-reduce.33.cloned.1.call-done = (bf16[128,384]{0,1:T(8,128)(2,1)}, bf16[128,384]{0,1:T(8,128)(2,1)}) async-done(((bf16[128,384]{0,1:T(8,128)(2,1)}, bf16[128,384]{0,1:T(8,128)(2,1)}), (bf16[128,384]{0,1:T(8,128)(2,1)}, bf16[128,384]{0,1:T(8,128)(2,1)})) %all-reduce.33.cloned.1.call-update) | async-done | bytes 196624 | tf_op jit(solution)/shard_map/psum | solution.py:12
  818.0 1.0 copy.45
  819.0 1.7 scatter_fusion.4
  821.4 1.5 fusion.13
  823.8 0.9 gather_fusion.5
  826.2 75.2 %all-reduce.29.cloned.1.call-done = bf16[128,384]{0,1:T(8,128)(2,1)} async-done(((bf16[128,384]{0,1:T(8,128)(2,1)}), bf16[128,384]{0,1:T(8,128)(2,1)}) %all-reduce.29.cloned.1.call-update) | async-done | bytes 98320 | tf_op jit(solution)/shard_map/psum | solution.py:32
  901.4 1.8 fusion.29
  903.2 49.0 %all-gather.5 = bf16[1,1536,128]{2,1,0:T(8,128)(2,1)S(1)} all-gather(bf16[1,24,128]{2,1,0:T(8,128)(2,1)S(1)} %get-tuple-element.102), channel_id=7, replica_groups=mesh['pa'=8,'pb'=64] {'pb'}, dimensions={1}, use_global_device_ids=true | all-gather | bytes 399360 | tf_op jit(solution)/shard_map/all_gather | solution.py:43
  952.2 27.4 %all-reduce.31.cloned.1.call-done = (bf16[128,384]{0,1:T(8,128)(2,1)}, bf16[128,384]{0,1:T(8,128)(2,1)}) async-done(((bf16[128,384]{0,1:T(8,128)(2,1)}, bf16[128,384]{0,1:T(8,128)(2,1)}), (bf16[128,384]{0,1:T(8,128)(2,1)}, bf16[128,384]{0,1:T(8,128)(2,1)})) %all-reduce.31.cloned.1.call-update) | async-done | bytes 196624 | tf_op jit(solution)/shard_map/psum | solution.py:12
  979.6 1.0 copy.51
  980.6 1.7 scatter_fusion.5
  983.8 1.4 copy.56
  (141 shorter events, 26.8 us)
Async XLA Ops:
  6.5 1.3 copy-start.10
  6.5 86.0 %all-reduce.19.cloned.1.call-start = ((), (), s32[]{:S(2)}) async-start(), calls=%async_computation | async-start | bytes 196608 | tf_op jit(solution)/shard_map/psum | solution.py:32
  7.8 5.5 copy-start.6
  10.7 160.2 %all-reduce.41.cloned.1.call-start = ((), (), s32[]{:S(2)}) async-start(), calls=%async_computation.11 | async-start | bytes 393216 | tf_op jit(solution)/shard_map/psum | solution.py:12
  94.3 160.1 %all-reduce.21.cloned.1.call-start = ((), (), s32[]{:S(2)}) async-start(), calls=%async_computation.1 | async-start | bytes 196608 | tf_op jit(solution)/shard_map/psum | solution.py:32
  174.3 1.5 copy-start
  175.9 1.9 copy-start.16
  175.9 1.9 copy-start.25
  176.7 79.5 %copy-start.9 = (bf16[1,24,128]{2,1,0:T(8,128)(2,1)S(1)}, bf16[1,24,128]{2,1,0:T(8,128)(2,1)}, u32[]{:S(2)}) copy-start(bf16[1,24,128]{2,1,0:T(8,128)(2,1)} %get-tuple-element.105) | copy-start | bytes 18436
  176.7 133.2 %copy-start.30 = (s32[128]{0:T(128)S(1)}, s32[128]{0:T(128)}, u32[]{:S(2)}) copy-start(s32[128]{0:T(128)} %get-tuple-element.119) | copy-start | bytes 1540
  176.7 156.9 %copy-start.26 = (s32[128]{0:T(128)S(1)}, s32[128]{0:T(128)}, u32[]{:S(2)}) copy-start(s32[128]{0:T(128)} %get-tuple-element.125) | copy-start | bytes 1540
  178.5 154.1 %all-reduce.39.cloned.1.call-start = ((), (), s32[]{:S(2)}) async-start(), calls=%async_computation.10 | async-start | bytes 393216 | tf_op jit(solution)/shard_map/psum | solution.py:12
  256.2 159.9 %all-reduce.23.cloned.1.call-start = ((), (), s32[]{:S(2)}) async-start(), calls=%async_computation.2 | async-start | bytes 196608 | tf_op jit(solution)/shard_map/psum | solution.py:32
  336.0 1.5 copy-start.2
  337.7 1.9 copy-start.15
  337.7 1.9 copy-start.23
  338.4 79.5 %copy-start.8 = (bf16[1,24,128]{2,1,0:T(8,128)(2,1)S(1)}, bf16[1,24,128]{2,1,0:T(8,128)(2,1)}, u32[]{:S(2)}) copy-start(bf16[1,24,128]{2,1,0:T(8,128)(2,1)} %get-tuple-element.104) | copy-start | bytes 18436
  338.4 133.3 %copy-start.29 = (s32[128]{0:T(128)S(1)}, s32[128]{0:T(128)}, u32[]{:S(2)}) copy-start(s32[128]{0:T(128)} %get-tuple-element.117) | copy-start | bytes 1540
  338.5 156.9 %copy-start.24 = (s32[128]{0:T(128)S(1)}, s32[128]{0:T(128)}, u32[]{:S(2)}) copy-start(s32[128]{0:T(128)} %get-tuple-element.126) | copy-start | bytes 1540
  340.3 154.1 %all-reduce.37.cloned.1.call-start = ((), (), s32[]{:S(2)}) async-start(), calls=%async_computation.9 | async-start | bytes 393216 | tf_op jit(solution)/shard_map/psum | solution.py:12
  417.9 159.9 %all-reduce.25.cloned.1.call-start = ((), (), s32[]{:S(2)}) async-start(), calls=%async_computation.3 | async-start | bytes 196608 | tf_op jit(solution)/shard_map/psum | solution.py:32
  497.8 1.5 copy-start.3
  499.4 1.9 copy-start.14
  499.4 1.9 copy-start.21
  500.2 79.5 %copy-start.7 = (bf16[1,24,128]{2,1,0:T(8,128)(2,1)S(1)}, bf16[1,24,128]{2,1,0:T(8,128)(2,1)}, u32[]{:S(2)}) copy-start(bf16[1,24,128]{2,1,0:T(8,128)(2,1)} %get-tuple-element.103) | copy-start | bytes 18436
  500.2 133.2 %copy-start.28 = (s32[128]{0:T(128)S(1)}, s32[128]{0:T(128)}, u32[]{:S(2)}) copy-start(s32[128]{0:T(128)} %get-tuple-element.115) | copy-start | bytes 1540
  500.2 157.1 %copy-start.22 = (s32[128]{0:T(128)S(1)}, s32[128]{0:T(128)}, u32[]{:S(2)}) copy-start(s32[128]{0:T(128)} %get-tuple-element.127) | copy-start | bytes 1540
  502.0 154.2 %all-reduce.35.cloned.1.call-start = ((), (), s32[]{:S(2)}) async-start(), calls=%async_computation.8 | async-start | bytes 393216 | tf_op jit(solution)/shard_map/psum | solution.py:12
  579.7 160.1 %all-reduce.27.cloned.1.call-start = ((), (), s32[]{:S(2)}) async-start(), calls=%async_computation.4 | async-start | bytes 196608 | tf_op jit(solution)/shard_map/psum | solution.py:32
  659.7 1.5 copy-start.4
  661.3 1.9 copy-start.13
  661.3 1.9 copy-start.19
  662.1 133.4 %copy-start.27 = (s32[128]{0:T(128)S(1)}, s32[128]{0:T(128)}, u32[]{:S(2)}) copy-start(s32[128]{0:T(128)} %get-tuple-element.91) | copy-start | bytes 1540
  662.1 156.9 %copy-start.20 = (s32[128]{0:T(128)S(1)}, s32[128]{0:T(128)}, u32[]{:S(2)}) copy-start(s32[128]{0:T(128)} %get-tuple-element.128) | copy-start | bytes 1540
  663.9 154.1 %all-reduce.33.cloned.1.call-start = ((), (), s32[]{:S(2)}) async-start(), calls=%async_computation.7 | async-start | bytes 393216 | tf_op jit(solution)/shard_map/psum | solution.py:12
  741.5 159.8 %all-reduce.29.cloned.1.call-start = ((), (), s32[]{:S(2)}) async-start(), calls=%async_computation.5 | async-start | bytes 196608 | tf_op jit(solution)/shard_map/psum | solution.py:32
  820.7 0.7 copy-start.11
  821.4 1.6 copy-start.5
  823.1 1.8 copy-start.12
  823.1 1.8 copy-start.17
  823.8 156.8 %copy-start.18 = (s32[128]{0:T(128)S(1)}, s32[128]{0:T(128)}, u32[]{:S(2)}) copy-start(s32[128]{0:T(128)} %get-tuple-element.124) | copy-start | bytes 1540
  825.5 154.1 %all-reduce.31.cloned.1.call-start = ((), (), s32[]{:S(2)}) async-start(), calls=%async_computation.6 | async-start | bytes 393216 | tf_op jit(solution)/shard_map/psum | solution.py:12
  982.4 0.9 copy-start.1
Sparse Core Ops, SparseCore 0:
  10.8 81.6 all-reduce.18
  95.0 75.9 all-reduce.40
  178.7 75.6 all-reduce.20
  256.7 75.9 all-reduce.38
  340.4 75.6 all-reduce.22
  418.4 75.9 all-reduce.36
  502.1 75.6 all-reduce.24
  580.3 75.9 all-reduce.34
  664.0 75.6 all-reduce.26
  742.0 75.9 all-reduce.32
  825.6 75.6 all-reduce.28
  903.7 75.9 all-reduce.30
where the time goes:
time: 993 us; the launch traced here: 992 us
  waiting for transfers between devices  588 us (59%)
  blocking collectives  321 us (32%)
  local copies, waits for them, and re-layouts  34.2 us (3%)
  matrix products  18.7 us (2%)
  other arithmetic  15.4 us (2%)
  between operations  14.3 us (1%)
    psum x6, waiting for transfers between devices, per_device(): lax.psum(candidates, 'pa').astype(jnp.float32).astype(jnp.bfloat16)  395 us
    all_gather x6, blocking collectives, per_device(): lax.all_gather(panels[step], 'pb', axis=0, tiled=True)  321 us
    psum x6, waiting for transfers between devices, broadcast(): return lax.psum(jnp.where(mine, x, jnp.zeros_like(x)), axis)  192 us
  transfers between devices with their start and end apart: 12, of which 12 were waited for; matrix products, arithmetic and copies ran while one was open for 1% of the time, Pallas kernels for 0%

commit v1 on v0

--- a/solution.py
+++ b/solution.py
@@ -40,7 +40,9 @@
         target = jnp.where(owned, local_idx, local_rows)
         matrix = matrix.at[target].set(old_top, mode="drop")
         product = jnp.dot(
-            lax.all_gather(panels[step], "pb", axis=0, tiled=True),
+            jnp.concatenate(
+                lax.all_to_all(jnp.stack([panels[step]] * lax.axis_size("pb")), "pb", 0, 0), axis=0
+            ),
             upper,
             preferred_element_type=jnp.float32,
         )

time: 993 us -> 1050 us (1.057)
  blocking collectives: 321 us -> 0 us
  waiting for transfers between devices: 588 us -> 892 us
  starting transfers between devices: 0.46 us -> 69.7 us
    all_gather x6 -> x0, blocking collectives: 321 us -> none  [per_device(): lax.all_gather(panels[step], 'pb', axis=0, tiled=True)]
    psum x6, waiting for transfers between devices: 192 us -> 455 us  [broadcast(): return lax.psum(jnp.where(mine, x, jnp.zeros_like(x)), axis)]
    all_to_all x0 -> x6, starting transfers between devices: none -> 69.2 us  [per_device(): lax.all_to_all(jnp.stack([panels[step]] * lax.axis_size('pb')), 'pb', 0, 0)]
    psum x6, waiting for transfers between devices: 395 us -> 437 us  [per_device(): lax.psum(candidates, 'pa').astype(jnp.float32).astype(jnp.bfloat16)]
  transfers between devices with their start and end apart: 12 -> 18, of which waited for: 12 -> 12; matrix products, arithmetic and copies ran while one was open for 1% -> 6% of each run, Pallas kernels for 0% -> 0%
where the time goes in v1:
time: 1050 us
  waiting for transfers between devices  892 us (85%)
  starting transfers between devices  69.7 us (7%)
  local copies, waits for them, and re-layouts  39.2 us (4%)
  matrix products  19.6 us (2%)
  other arithmetic  15.1 us (1%)
  between operations  14.4 us (1%)
    psum x6, waiting for transfers between devices, broadcast(): return lax.psum(jnp.where(mine, x, jnp.zeros_like(x)), axis)  455 us
    psum x6, waiting for transfers between devices, per_device(): lax.psum(candidates, 'pa').astype(jnp.float32).astype(jnp.bfloat16)  437 us
    all_to_all x6, starting transfers between devices, per_device(): lax.all_to_all(jnp.stack([panels[step]] * lax.axis_size('pb')), 'pb', 0, 0)  69.2 us
  transfers between devices with their start and end apart: 18, of which 12 were waited for; matrix products, arithmetic and copies ran while one was open for 6% of the time, Pallas kernels for 0%

profile of v1, /device:TPU:2, one launch (start us, length us, event | category | flops | bytes accessed | tf_op | source)
XLA Modules:
  0.0 1050.0 jit_solution(5168729202979254448)
XLA Ops:
  6.5 1.3 copy.89
  12.1 13.9 %all-to-all-start = ((bf16[64,24,128]{2,1,0:T(8,128)(2,1)}), bf16[64,24,128]{2,1,0:T(8,128)(2,1)S(1)}, u32[]{:S(2)}, u32[]{:S(2)}) async-start(bf16[64,24,128]{2,1,0:T(8,128)(2,1)} %stack.18), calls=%async_computation | async-start | bytes 786432 | tf_op jit(solution)/shard_map/all_to_all | solution.py:44
  28.1 64.5 %all-reduce.19.cloned.1.call-done = bf16[128,384]{0,1:T(8,128)(2,1)} async-done(((bf16[128,384]{0,1:T(8,128)(2,1)}), bf16[128,384]{0,1:T(8,128)(2,1)}) %all-reduce.19.cloned.1.call-update) | async-done | bytes 98320 | tf_op jit(solution)/shard_map/psum | solution.py:32
  92.5 1.8 fusion.19
  95.0 76.0 %all-reduce.41.cloned.1.call-done = (bf16[128,384]{0,1:T(8,128)(2,1)}, bf16[128,384]{0,1:T(8,128)(2,1)}) async-done(((bf16[128,384]{0,1:T(8,128)(2,1)}, bf16[128,384]{0,1:T(8,128)(2,1)}), (bf16[128,384]{0,1:T(8,128)(2,1)}, bf16[128,384]{0,1:T(8,128)(2,1)})) %all-reduce.41.cloned.1.call-update) | async-done | bytes 196624 | tf_op jit(solution)/shard_map/psum | solution.py:12
  170.9 1.0 copy.22
  171.9 1.7 scatter_fusion
  175.2 11.1 %all-to-all-start.1 = ((bf16[64,24,128]{2,1,0:T(8,128)(2,1)}), bf16[64,24,128]{2,1,0:T(8,128)(2,1)}, u32[]{:S(2)}, u32[]{:S(2)}) async-start(bf16[64,24,128]{2,1,0:T(8,128)(2,1)} %stack.19), calls=%async_computation.1 | async-start | bytes 786432 | tf_op jit(solution)/shard_map/all_to_all | solution.py:44
  186.3 1.5 fusion.17
  188.7 1.0 gather_fusion.1
  191.2 74.5 %all-reduce.21.cloned.1.call-done = bf16[128,384]{0,1:T(8,128)(2,1)} async-done(((bf16[128,384]{0,1:T(8,128)(2,1)}), bf16[128,384]{0,1:T(8,128)(2,1)}) %all-reduce.21.cloned.1.call-update) | async-done | bytes 98320 | tf_op jit(solution)/shard_map/psum | solution.py:32
  265.7 1.8 fusion.21
  268.8 75.2 %all-reduce.39.cloned.1.call-done = (bf16[128,384]{0,1:T(8,128)(2,1)}, bf16[128,384]{0,1:T(8,128)(2,1)}) async-done(((bf16[128,384]{0,1:T(8,128)(2,1)}, bf16[128,384]{0,1:T(8,128)(2,1)}), (bf16[128,384]{0,1:T(8,128)(2,1)}, bf16[128,384]{0,1:T(8,128)(2,1)})) %all-reduce.39.cloned.1.call-update) | async-done | bytes 196624 | tf_op jit(solution)/shard_map/psum | solution.py:12
  344.0 1.0 copy.27
  345.0 1.7 scatter_fusion.1
  348.2 11.1 %all-to-all-start.2 = ((bf16[64,24,128]{2,1,0:T(8,128)(2,1)}), bf16[64,24,128]{2,1,0:T(8,128)(2,1)}, u32[]{:S(2)}, u32[]{:S(2)}) async-start(bf16[64,24,128]{2,1,0:T(8,128)(2,1)} %stack.20), calls=%async_computation.2 | async-start | bytes 786432 | tf_op jit(solution)/shard_map/all_to_all | solution.py:44
  359.4 1.5 fusion.16
  361.7 1.0 gather_fusion.2
  364.3 74.5 %all-reduce.23.cloned.1.call-done = bf16[128,384]{0,1:T(8,128)(2,1)} async-done(((bf16[128,384]{0,1:T(8,128)(2,1)}), bf16[128,384]{0,1:T(8,128)(2,1)}) %all-reduce.23.cloned.1.call-update) | async-done | bytes 98320 | tf_op jit(solution)/shard_map/psum | solution.py:32
  438.8 1.8 fusion.23
  441.8 75.2 %all-reduce.37.cloned.1.call-done = (bf16[128,384]{0,1:T(8,128)(2,1)}, bf16[128,384]{0,1:T(8,128)(2,1)}) async-done(((bf16[128,384]{0,1:T(8,128)(2,1)}, bf16[128,384]{0,1:T(8,128)(2,1)}), (bf16[128,384]{0,1:T(8,128)(2,1)}, bf16[128,384]{0,1:T(8,128)(2,1)})) %all-reduce.37.cloned.1.call-update) | async-done | bytes 196624 | tf_op jit(solution)/shard_map/psum | solution.py:12
  517.0 1.0 copy.33
  518.1 1.9 scatter_fusion.2
  521.5 11.1 %all-to-all-start.3 = ((bf16[64,24,128]{2,1,0:T(8,128)(2,1)}), bf16[64,24,128]{2,1,0:T(8,128)(2,1)}, u32[]{:S(2)}, u32[]{:S(2)}) async-start(bf16[64,24,128]{2,1,0:T(8,128)(2,1)} %stack.21), calls=%async_computation.3 | async-start | bytes 786432 | tf_op jit(solution)/shard_map/all_to_all | solution.py:44
  532.6 1.5 fusion.15
  535.0 1.0 gather_fusion.3
  537.5 74.6 %all-reduce.25.cloned.1.call-done = bf16[128,384]{0,1:T(8,128)(2,1)} async-done(((bf16[128,384]{0,1:T(8,128)(2,1)}), bf16[128,384]{0,1:T(8,128)(2,1)}) %all-reduce.25.cloned.1.call-update) | async-done | bytes 98320 | tf_op jit(solution)/shard_map/psum | solution.py:32
  612.1 1.8 fusion.25
  615.1 75.4 %all-reduce.35.cloned.1.call-done = (bf16[128,384]{0,1:T(8,128)(2,1)}, bf16[128,384]{0,1:T(8,128)(2,1)}) async-done(((bf16[128,384]{0,1:T(8,128)(2,1)}, bf16[128,384]{0,1:T(8,128)(2,1)}), (bf16[128,384]{0,1:T(8,128)(2,1)}, bf16[128,384]{0,1:T(8,128)(2,1)})) %all-reduce.35.cloned.1.call-update) | async-done | bytes 196624 | tf_op jit(solution)/shard_map/psum | solution.py:12
  690.5 1.0 copy.39
  691.5 1.7 scatter_fusion.3
  694.7 11.1 %all-to-all-start.4 = ((bf16[64,24,128]{2,1,0:T(8,128)(2,1)}), bf16[64,24,128]{2,1,0:T(8,128)(2,1)}, u32[]{:S(2)}, u32[]{:S(2)}) async-start(bf16[64,24,128]{2,1,0:T(8,128)(2,1)} %stack.22), calls=%async_computation.4 | async-start | bytes 786432 | tf_op jit(solution)/shard_map/all_to_all | solution.py:44
  705.9 1.5 fusion.14
  708.2 1.0 gather_fusion.4
  710.8 74.6 %all-reduce.27.cloned.1.call-done = bf16[128,384]{0,1:T(8,128)(2,1)} async-done(((bf16[128,384]{0,1:T(8,128)(2,1)}), bf16[128,384]{0,1:T(8,128)(2,1)}) %all-reduce.27.cloned.1.call-update) | async-done | bytes 98320 | tf_op jit(solution)/shard_map/psum | solution.py:32
  785.4 1.8 fusion.27
  787.2 76.4 %all-reduce.33.cloned.1.call-done = (bf16[128,384]{0,1:T(8,128)(2,1)}, bf16[128,384]{0,1:T(8,128)(2,1)}) async-done(((bf16[128,384]{0,1:T(8,128)(2,1)}, bf16[128,384]{0,1:T(8,128)(2,1)}), (bf16[128,384]{0,1:T(8,128)(2,1)}, bf16[128,384]{0,1:T(8,128)(2,1)})) %all-reduce.33.cloned.1.call-update) | async-done | bytes 196624 | tf_op jit(solution)/shard_map/psum | solution.py:12
  863.6 1.0 copy.45
  864.6 1.7 scatter_fusion.4
  867.8 11.1 %all-to-all-start.5 = ((bf16[64,24,128]{2,1,0:T(8,128)(2,1)}), bf16[64,24,128]{2,1,0:T(8,128)(2,1)}, u32[]{:S(2)}, u32[]{:S(2)}) async-start(bf16[64,24,128]{2,1,0:T(8,128)(2,1)} %stack.23), calls=%async_computation.5 | async-start | bytes 786432 | tf_op jit(solution)/shard_map/all_to_all | solution.py:44
  879.0 1.5 fusion.13
  883.7 74.5 %all-reduce.29.cloned.1.call-done = bf16[128,384]{0,1:T(8,128)(2,1)} async-done(((bf16[128,384]{0,1:T(8,128)(2,1)}), bf16[128,384]{0,1:T(8,128)(2,1)}) %all-reduce.29.cloned.1.call-update) | async-done | bytes 98320 | tf_op jit(solution)/shard_map/psum | solution.py:32
  958.2 1.8 fusion.29
  960.1 76.4 %all-reduce.31.cloned.1.call-done = (bf16[128,384]{0,1:T(8,128)(2,1)}, bf16[128,384]{0,1:T(8,128)(2,1)}) async-done(((bf16[128,384]{0,1:T(8,128)(2,1)}, bf16[128,384]{0,1:T(8,128)(2,1)}), (bf16[128,384]{0,1:T(8,128)(2,1)}, bf16[128,384]{0,1:T(8,128)(2,1)})) %all-reduce.31.cloned.1.call-update) | async-done | bytes 196624 | tf_op jit(solution)/shard_map/psum | solution.py:12
  1036.5 1.0 copy.51
  1037.5 1.7 scatter_fusion.5
  1040.1 1.5 fusion.12
  1041.7 1.4 copy.56
  (159 shorter events, 31.6 us)
Async XLA Ops:
  6.5 86.0 %all-reduce.19.cloned.1.call-start = ((), (), s32[]{:S(2)}) async-start(), calls=%async_computation.6 | async-start | bytes 196608 | tf_op jit(solution)/shard_map/psum | solution.py:32
  7.8 2.9 copy-start.7
  12.1 162.2 %all-to-all-start = ((bf16[64,24,128]{2,1,0:T(8,128)(2,1)}), bf16[64,24,128]{2,1,0:T(8,128)(2,1)S(1)}, u32[]{:S(2)}, u32[]{:S(2)}) async-start(bf16[64,24,128]{2,1,0:T(8,128)(2,1)} %stack.18), calls=%async_computation | async-start | bytes 786432 | tf_op jit(solution)/shard_map/all_to_all | solution.py:44
  26.0 144.9 %all-reduce.41.cloned.1.call-start = ((), (), s32[]{:S(2)}) async-start(), calls=%async_computation.17 | async-start | bytes 393216 | tf_op jit(solution)/shard_map/psum | solution.py:12
  174.3 12.0 %copy-start.1 = (bf16[128,384]{0,1:T(8,128)(2,1)S(1)}, bf16[128,384]{0,1:T(8,128)(2,1)}, u32[]{:S(2)}) copy-start(bf16[128,384]{0,1:T(8,128)(2,1)} %get-tuple-element.89) | copy-start | bytes 294916
  174.3 12.0 %copy-start.11 = (pred[1536]{0:T(1024)(128)(4,1)S(1)}, pred[1536]{0:T(1024)(128)(4,1)}, u32[]{:S(2)}) copy-start(pred[1536]{0:T(1024)(128)(4,1)} %fusion.48) | copy-start | bytes 4612
  174.4 11.9 %copy-start = (bf16[64,24,128]{2,1,0:T(8,128)(2,1)}, bf16[64,24,128]{2,1,0:T(8,128)(2,1)S(1)}, u32[]{:S(2)}) copy-start(bf16[64,24,128]{2,1,0:T(8,128)(2,1)S(1)} %all-to-all-done) | copy-start | bytes 1179652
  175.2 172.3 %all-to-all-start.1 = ((bf16[64,24,128]{2,1,0:T(8,128)(2,1)}), bf16[64,24,128]{2,1,0:T(8,128)(2,1)}, u32[]{:S(2)}, u32[]{:S(2)}) async-start(bf16[64,24,128]{2,1,0:T(8,128)(2,1)} %stack.19), calls=%async_computation.1 | async-start | bytes 786432 | tf_op jit(solution)/shard_map/all_to_all | solution.py:44
  186.2 79.5 %all-reduce.21.cloned.1.call-start = ((), (), s32[]{:S(2)}) async-start(), calls=%async_computation.7 | async-start | bytes 196608 | tf_op jit(solution)/shard_map/psum | solution.py:32
  187.9 1.9 copy-start.19
  187.9 1.9 copy-start.28
  188.6 79.5 %copy-start.33 = (s32[128]{0:T(128)S(1)}, s32[128]{0:T(128)}, u32[]{:S(2)}) copy-start(s32[128]{0:T(128)} %get-tuple-element.119) | copy-start | bytes 1540
  188.7 156.3 %copy-start.29 = (s32[128]{0:T(128)S(1)}, s32[128]{0:T(128)}, u32[]{:S(2)}) copy-start(s32[128]{0:T(128)} %get-tuple-element.125) | copy-start | bytes 1540
  190.5 153.5 %all-reduce.39.cloned.1.call-start = ((), (), s32[]{:S(2)}) async-start(), calls=%async_computation.16 | async-start | bytes 393216 | tf_op jit(solution)/shard_map/psum | solution.py:12
  347.4 12.0 %copy-start.3 = (bf16[128,384]{0,1:T(8,128)(2,1)S(1)}, bf16[128,384]{0,1:T(8,128)(2,1)}, u32[]{:S(2)}) copy-start(bf16[128,384]{0,1:T(8,128)(2,1)} %get-tuple-element.87) | copy-start | bytes 294916
  347.4 12.0 %copy-start.12 = (pred[1536]{0:T(1024)(128)(4,1)S(1)}, pred[1536]{0:T(1024)(128)(4,1)}, u32[]{:S(2)}) copy-start(pred[1536]{0:T(1024)(128)(4,1)} %fusion.49) | copy-start | bytes 4612
  348.2 172.4 %all-to-all-start.2 = ((bf16[64,24,128]{2,1,0:T(8,128)(2,1)}), bf16[64,24,128]{2,1,0:T(8,128)(2,1)}, u32[]{:S(2)}, u32[]{:S(2)}) async-start(bf16[64,24,128]{2,1,0:T(8,128)(2,1)} %stack.20), calls=%async_computation.2 | async-start | bytes 786432 | tf_op jit(solution)/shard_map/all_to_all | solution.py:44
  359.3 79.5 %all-reduce.23.cloned.1.call-start = ((), (), s32[]{:S(2)}) async-start(), calls=%async_computation.8 | async-start | bytes 196608 | tf_op jit(solution)/shard_map/psum | solution.py:32
  360.9 1.9 copy-start.18
  361.0 1.9 copy-start.26
  361.7 79.5 %copy-start.32 = (s32[128]{0:T(128)S(1)}, s32[128]{0:T(128)}, u32[]{:S(2)}) copy-start(s32[128]{0:T(128)} %get-tuple-element.117) | copy-start | bytes 1540
  361.7 156.3 %copy-start.27 = (s32[128]{0:T(128)S(1)}, s32[128]{0:T(128)}, u32[]{:S(2)}) copy-start(s32[128]{0:T(128)} %get-tuple-element.126) | copy-start | bytes 1540
  363.5 153.5 %all-reduce.37.cloned.1.call-start = ((), (), s32[]{:S(2)}) async-start(), calls=%async_computation.15 | async-start | bytes 393216 | tf_op jit(solution)/shard_map/psum | solution.py:12
  520.6 12.0 %copy-start.4 = (bf16[128,384]{0,1:T(8,128)(2,1)S(1)}, bf16[128,384]{0,1:T(8,128)(2,1)}, u32[]{:S(2)}) copy-start(bf16[128,384]{0,1:T(8,128)(2,1)} %get-tuple-element.85) | copy-start | bytes 294916
  520.7 12.0 %copy-start.13 = (pred[1536]{0:T(1024)(128)(4,1)S(1)}, pred[1536]{0:T(1024)(128)(4,1)}, u32[]{:S(2)}) copy-start(pred[1536]{0:T(1024)(128)(4,1)} %fusion.50) | copy-start | bytes 4612
  521.5 172.4 %all-to-all-start.3 = ((bf16[64,24,128]{2,1,0:T(8,128)(2,1)}), bf16[64,24,128]{2,1,0:T(8,128)(2,1)}, u32[]{:S(2)}, u32[]{:S(2)}) async-start(bf16[64,24,128]{2,1,0:T(8,128)(2,1)} %stack.21), calls=%async_computation.3 | async-start | bytes 786432 | tf_op jit(solution)/shard_map/all_to_all | solution.py:44
  532.6 79.5 %all-reduce.25.cloned.1.call-start = ((), (), s32[]{:S(2)}) async-start(), calls=%async_computation.9 | async-start | bytes 196608 | tf_op jit(solution)/shard_map/psum | solution.py:32
  534.2 1.9 copy-start.17
  534.2 1.9 copy-start.24
  534.9 79.6 %copy-start.31 = (s32[128]{0:T(128)S(1)}, s32[128]{0:T(128)}, u32[]{:S(2)}) copy-start(s32[128]{0:T(128)} %get-tuple-element.115) | copy-start | bytes 1540
  535.0 156.5 %copy-start.25 = (s32[128]{0:T(128)S(1)}, s32[128]{0:T(128)}, u32[]{:S(2)}) copy-start(s32[128]{0:T(128)} %get-tuple-element.127) | copy-start | bytes 1540
  536.8 153.7 %all-reduce.35.cloned.1.call-start = ((), (), s32[]{:S(2)}) async-start(), calls=%async_computation.14 | async-start | bytes 393216 | tf_op jit(solution)/shard_map/psum | solution.py:12
  693.9 12.0 %copy-start.5 = (bf16[128,384]{0,1:T(8,128)(2,1)S(1)}, bf16[128,384]{0,1:T(8,128)(2,1)}, u32[]{:S(2)}) copy-start(bf16[128,384]{0,1:T(8,128)(2,1)} %get-tuple-element.83) | copy-start | bytes 294916
  693.9 12.0 %copy-start.14 = (pred[1536]{0:T(1024)(128)(4,1)S(1)}, pred[1536]{0:T(1024)(128)(4,1)}, u32[]{:S(2)}) copy-start(pred[1536]{0:T(1024)(128)(4,1)} %fusion.51) | copy-start | bytes 4612
  694.7 172.3 %all-to-all-start.4 = ((bf16[64,24,128]{2,1,0:T(8,128)(2,1)}), bf16[64,24,128]{2,1,0:T(8,128)(2,1)}, u32[]{:S(2)}, u32[]{:S(2)}) async-start(bf16[64,24,128]{2,1,0:T(8,128)(2,1)} %stack.22), calls=%async_computation.4 | async-start | bytes 786432 | tf_op jit(solution)/shard_map/all_to_all | solution.py:44
  705.8 79.5 %all-reduce.27.cloned.1.call-start = ((), (), s32[]{:S(2)}) async-start(), calls=%async_computation.10 | async-start | bytes 196608 | tf_op jit(solution)/shard_map/psum | solution.py:32
  707.4 1.9 copy-start.16
  707.5 1.9 copy-start.22
  708.2 79.0 %copy-start.30 = (s32[128]{0:T(128)S(1)}, s32[128]{0:T(128)}, u32[]{:S(2)}) copy-start(s32[128]{0:T(128)} %get-tuple-element.91) | copy-start | bytes 1540
  708.2 156.4 %copy-start.23 = (s32[128]{0:T(128)S(1)}, s32[128]{0:T(128)}, u32[]{:S(2)}) copy-start(s32[128]{0:T(128)} %get-tuple-element.128) | copy-start | bytes 1540
  710.0 153.5 %all-reduce.33.cloned.1.call-start = ((), (), s32[]{:S(2)}) async-start(), calls=%async_computation.13 | async-start | bytes 393216 | tf_op jit(solution)/shard_map/psum | solution.py:12
  867.0 11.9 %copy-start.2 = (bf16[128,384]{0,1:T(8,128)(2,1)S(1)}, bf16[128,384]{0,1:T(8,128)(2,1)}, u32[]{:S(2)}) copy-start(bf16[128,384]{0,1:T(8,128)(2,1)} %get-tuple-element.81) | copy-start | bytes 294916
  867.8 172.1 %all-to-all-start.5 = ((bf16[64,24,128]{2,1,0:T(8,128)(2,1)}), bf16[64,24,128]{2,1,0:T(8,128)(2,1)}, u32[]{:S(2)}, u32[]{:S(2)}) async-start(bf16[64,24,128]{2,1,0:T(8,128)(2,1)} %stack.23), calls=%async_computation.5 | async-start | bytes 786432 | tf_op jit(solution)/shard_map/all_to_all | solution.py:44
  878.9 79.3 %all-reduce.29.cloned.1.call-start = ((), (), s32[]{:S(2)}) async-start(), calls=%async_computation.11 | async-start | bytes 196608 | tf_op jit(solution)/shard_map/psum | solution.py:32
  880.5 1.8 copy-start.15
  880.5 1.8 copy-start.20
  881.3 156.2 %copy-start.21 = (s32[128]{0:T(128)S(1)}, s32[128]{0:T(128)}, u32[]{:S(2)}) copy-start(s32[128]{0:T(128)} %get-tuple-element.124) | copy-start | bytes 1540
  883.0 153.5 %all-reduce.31.cloned.1.call-start = ((), (), s32[]{:S(2)}) async-start(), calls=%async_computation.12 | async-start | bytes 393216 | tf_op jit(solution)/shard_map/psum | solution.py:12
  (4 other events, 3.6 us)
Sparse Core Ops, SparseCore 0:
  10.8 81.6 all-reduce.18
  95.0 75.9 all-reduce.40
  190.6 75.0 all-reduce.20
  268.0 75.9 all-reduce.38
  363.7 75.0 all-reduce.22
  441.1 75.9 all-reduce.36
  536.9 75.1 all-reduce.24
  614.5 75.9 all-reduce.34
  710.2 75.1 all-reduce.26
  787.6 75.9 all-reduce.32
  883.1 75.0 all-reduce.28
  960.5 75.9 all-reduce.30
